TPU v7x, 256 devices: a whole 4x4x8 slice. The times are simulated.
256 devices in a mesh: replica: 2 (over z_lo), segment: 4 (over z_hi), tensor: 32 (over x, y, core).
Axes of the slice: x: 4, y: 4, z: 8 (z_hi: 4, z_lo: 2; z = z_hi * 2 + z_lo), core: 2. Of those that a mesh axis runs over, the one named last changes fastest.
Arguments:
- x_in: bfloat16 [256, 8192], P('replica', 'tensor'), parts along dimension 0, may hold values from -6 to 6
- norm_gain: float32 [4, 8192], P('segment'), may hold values from 0.5 to 1.5
- in_index: int32 [4, 224, 72], P('segment', 'tensor'), may hold values from -1 to 127, as said below
- gate_blocks: bfloat16 [4, 224, 72, 4096], P('segment', 'tensor'), may hold values from -0.09375 to 0.09375
- up_blocks: bfloat16 [4, 224, 72, 4096], P('segment', 'tensor'), may hold values from -0.09375 to 0.09375
- out_index: int32 [4, 128, 126], P('segment', 'tensor'), may hold values from -1 to 223, as said below
- down_blocks: bfloat16 [4, 128, 126, 4096], P('segment', 'tensor'), may hold values from -0.0625 to 0.0625
Outputs:
- sections: bfloat16 [4, 256, 8192], P('segment', 'replica', 'tensor'), parts along dimension 1
There are 2 independent parts, one for each index of `replica`. A program takes and returns all parts, laid end to end along the dimension named above; an argument that names none is the same for every part. Nothing has to cross between parts.
Inputs may be any that keep to these rules, and one draw needn't show every extreme that they name: `in_index`: for each section and column block the entries name distinct row blocks, the kept ones first and -1 in the remaining slots; between 3 * 128 / 8 (rounded down) and 72 slots are kept, and in every section some column block keeps exactly 72 and another exactly the least. `out_index`: for each section and column block the entries name distinct row blocks, the kept ones first and -1 in the remaining slots; between 3 * 224 / 8 (rounded down) and 126 slots are kept, and in every section some column block keeps exactly 126 and another exactly the least.
All inputs are finite; a program needn't handle non-finite values.
Results may differ from a plain program's by a relative error of at most 0.0095.
Values may be sent and summed in bfloat16 or wider, within the bound.
No kernel may reach another device: no remote copies, remote signals or barrier semaphores. Data moves between devices by JAX's collectives and lax.ppermute only.
A program may use at most 128 MiB of HBM per device.

v0:
```python
import jax
import jax.numpy as jnp
from jax import lax
from jax.sharding import PartitionSpec as P

D = 8192
FFW = 14336
BS = 64


def shifted(value, axis, by):
    length = lax.axis_size(axis)
    pairs = [(i, i + by) for i in range(length) if 0 <= i + by < length]
    return lax.ppermute(value, axis, pairs)


def densify(index, blocks, row_blocks):
    tile_count = index.shape[0]
    picks = (index[:, None, :] == jnp.arange(row_blocks, dtype=jnp.int32)[None, :, None]).astype(
        jnp.bfloat16
    )
    dense = jnp.einsum("crm,cmq->crq", picks, blocks, preferred_element_type=jnp.bfloat16)
    dense = dense.reshape(tile_count, row_blocks, BS, BS)
    return jnp.transpose(dense, (1, 2, 0, 3)).reshape(row_blocks * BS, tile_count * BS)


def local(x_in, norm_gain, in_index, gate_blocks, up_blocks, out_index, down_blocks):
    segment_count = lax.axis_size("segment")
    segment_at = lax.axis_index("segment")
    tokens, local_cols = x_in.shape
    gain_row = norm_gain[0]
    index_in = in_index[0]
    index_out = out_index[0]
    gate_dense = densify(index_in, gate_blocks[0], D // BS)
    up_dense = densify(index_in, up_blocks[0], D // BS)
    down_dense = densify(index_out, down_blocks[0], FFW // BS)
    rows_micro = tokens // 2
    group_count = tokens // rows_micro
    tick_count = group_count + segment_count - 1
    result = jnp.zeros((tokens, local_cols), jnp.bfloat16)
    carried = jnp.zeros((rows_micro, local_cols), jnp.bfloat16)
    for tick_now in range(tick_count):
        first_group = min(tick_now, group_count - 1)
        first_rows = x_in[first_group * rows_micro : (first_group + 1) * rows_micro]
        incoming = jnp.where(segment_at == 0, first_rows, carried)
        whole = lax.all_gather(incoming, "tensor", axis=1, tiled=True)
        wide = whole.astype(jnp.float32)
        stat = jnp.mean(wide * wide, axis=1, keepdims=True)
        section_normed = (wide * lax.rsqrt(stat + 1e-05) * gain_row[None, :]).astype(jnp.bfloat16)
        gate = jnp.dot(section_normed, gate_dense, preferred_element_type=jnp.float32)
        up_part = jnp.dot(section_normed, up_dense, preferred_element_type=jnp.float32)
        section_hidden = (jax.nn.silu(gate) * up_part).astype(jnp.bfloat16)
        mixed = jnp.dot(
            lax.all_gather(section_hidden, "tensor", axis=1, tiled=True),
            down_dense,
            preferred_element_type=jnp.float32,
        )
        produced = (incoming.astype(jnp.float32) + mixed).astype(jnp.bfloat16)
        micro_id = tick_now - segment_at
        is_valid = jnp.logical_and(micro_id >= 0, micro_id < group_count)
        offset = jnp.clip(micro_id, 0, group_count - 1) * rows_micro
        previous = lax.dynamic_slice_in_dim(result, offset, rows_micro, 0)
        result = lax.dynamic_update_slice_in_dim(
            result, jnp.where(is_valid, produced, previous), offset, 0
        )
        if tick_now + 1 < tick_count:
            carried = shifted(produced, "segment", 1)
    return result[None]


def solution(mesh):
    placed = (
        P("replica", "tensor"),
        P("segment", None),
        P("segment", "tensor", None),
        P("segment", "tensor", None, None),
        P("segment", "tensor", None, None),
        P("segment", "tensor", None),
        P("segment", "tensor", None, None),
    )
    return jax.shard_map(
        local,
        mesh=mesh,
        in_specs=placed,
        out_specs=P("segment", "replica", "tensor"),
        check_vma=False,
    )
```

profile of v0, /device:TPU:1, one launch (start us, length us, event | category | flops | bytes accessed | tf_op | source)
XLA Modules:
  0.0 696.2 jit_solution(13553117329584117888)
XLA Ops:
  8.7 7.7 %fusion.4 = bf16[7,128,4096]{1,2,0:T(8,128)(2,1)} fusion(bf16[1,7,72,4096]{3,2,1,0:T(8,128)(2,1)} %param.10, s32[7,72]{1,0:T(8,128)S(1)} %bitcast.103), kind=kOutput, calls=%fused_computation.4 | convolution fusion | flops 528546816 | bytes 11470816 | tf_op jit(solution)/shard_map/crm,cmq->crq/dot_general | solution.py:22
  16.4 15.6 %copy.22 = bf16[128,64,7,64]{1,0,3,2:T(8,128)(2,1)} copy(bf16[128,64,7,64]{0,3,1,2:T(8,128)(2,1)} %bitcast.90) | data formatting | bytes 14680064 | tf_op jit(solution)/shard_map/transpose | solution.py:24
  32.0 20.0 %reshape.63 = bf16[8192,448]{0,1:T(8,128)(2,1)} reshape(bf16[128,64,7,64]{1,0,3,2:T(8,128)(2,1)} %copy.22) | data formatting | bytes 14680064 | tf_op jit(solution)/shard_map/reshape | solution.py:24
  52.0 7.7 %fusion.2 = bf16[7,128,4096]{1,2,0:T(8,128)(2,1)} fusion(bf16[1,7,72,4096]{3,2,1,0:T(8,128)(2,1)} %param.11, s32[7,72]{1,0:T(8,128)S(1)} %bitcast.104), kind=kOutput, calls=%fused_computation.2 | convolution fusion | flops 528546816 | bytes 11470816 | tf_op jit(solution)/shard_map/crm,cmq->crq/dot_general | solution.py:22
  59.7 15.6 %copy.24 = bf16[128,64,7,64]{1,0,3,2:T(8,128)(2,1)} copy(bf16[128,64,7,64]{0,3,1,2:T(8,128)(2,1)} %bitcast.89) | data formatting | bytes 14680064 | tf_op jit(solution)/shard_map/transpose | solution.py:24
  75.3 20.0 %reshape.65 = bf16[8192,448]{0,1:T(8,128)(2,1)} reshape(bf16[128,64,7,64]{1,0,3,2:T(8,128)(2,1)} %copy.24) | data formatting | bytes 14680064 | tf_op jit(solution)/shard_map/reshape | solution.py:24
  96.9 5.8 fusion.41
  105.9 9.4 %fusion = bf16[4,224,4096]{1,2,0:T(8,128)(2,1)} fusion(bf16[4,126,4096]{2,0,1:T(4,128)(2,1)} %bitcast.91, s32[4,126]{1,0:T(4,128)S(1)} %bitcast.105), kind=kOutput, calls=%fused_computation | convolution fusion | flops 924956928 | bytes 11470816 | tf_op jit(solution)/shard_map/crm,cmq->crq/dot_general | solution.py:22
  115.3 17.4 %copy.28 = bf16[224,64,4,64]{1,0,3,2:T(8,128)(2,1)} copy(bf16[224,64,4,64]{0,3,1,2:T(8,128)(2,1)} %bitcast.88) | data formatting | bytes 14680064 | tf_op jit(solution)/shard_map/transpose | solution.py:24
  132.7 18.5 %reshape.67 = bf16[14336,256]{0,1:T(8,128)(2,1)} reshape(bf16[224,64,4,64]{1,0,3,2:T(8,128)(2,1)} %copy.28) | data formatting | bytes 14680064 | tf_op jit(solution)/shard_map/reshape | solution.py:24
  151.2 7.3 %all-gather.26.cloned.1.call-done = bf16[32,448,64]{1,2,0:T(8,128)(2,1)} async-done(((bf16[1,448,64]{1,2,0:T(8,128)(2,1)}), bf16[32,448,64]{1,2,0:T(8,128)(2,1)}) %all-gather.26.cloned.1.call-update) | async-done | bytes 1835024 | tf_op jit(solution)/shard_map/all_gather | solution.py:54
  164.7 6.0 select_dynamic-update-slice_fusion.3
  176.8 49.8 %all-gather.18.cloned.1.call-done = bf16[64,8192]{1,0:T(8,128)(2,1)} async-done(((bf16[64,256]{1,0:T(8,128)(2,1)}), bf16[64,8192]{1,0:T(8,128)(2,1)}) %all-gather.18.cloned.1.call-update) | async-done | bytes 1048592 | tf_op jit(solution)/shard_map/all_gather | solution.py:46
  228.2 5.7 fusion.38
  233.9 6.0 fusion.46
  240.0 48.1 %all-gather.28.cloned.1.call-done = bf16[32,448,64]{1,2,0:T(8,128)(2,1)} async-done(((bf16[1,448,64]{1,2,0:T(8,128)(2,1)}), bf16[32,448,64]{1,2,0:T(8,128)(2,1)}) %all-gather.28.cloned.1.call-update) | async-done | bytes 1835024 | tf_op jit(solution)/shard_map/all_gather | solution.py:54
  294.2 6.0 select_dynamic-update-slice_fusion.2
  306.0 50.0 %all-gather.20.cloned.1.call-done = bf16[64,8192]{1,0:T(8,128)(2,1)} async-done(((bf16[64,256]{1,0:T(8,128)(2,1)}), bf16[64,8192]{1,0:T(8,128)(2,1)}) %all-gather.20.cloned.1.call-update) | async-done | bytes 1048592 | tf_op jit(solution)/shard_map/all_gather | solution.py:46
  357.6 5.7 fusion.34
  363.4 6.0 fusion.47
  369.8 47.7 %all-gather.30.cloned.1.call-done = bf16[32,448,64]{1,2,0:T(8,128)(2,1)} async-done(((bf16[1,448,64]{1,2,0:T(8,128)(2,1)}), bf16[32,448,64]{1,2,0:T(8,128)(2,1)}) %all-gather.30.cloned.1.call-update) | async-done | bytes 1835024 | tf_op jit(solution)/shard_map/all_gather | solution.py:54
  423.7 6.0 select_dynamic-update-slice_fusion.1
  435.5 50.0 %all-gather.22.cloned.1.call-done = bf16[64,8192]{1,0:T(8,128)(2,1)} async-done(((bf16[64,256]{1,0:T(8,128)(2,1)}), bf16[64,8192]{1,0:T(8,128)(2,1)}) %all-gather.22.cloned.1.call-update) | async-done | bytes 1048592 | tf_op jit(solution)/shard_map/all_gather | solution.py:46
  487.1 5.7 fusion.30
  492.9 6.0 fusion.48
  498.9 48.1 %all-gather.32.cloned.1.call-done = bf16[32,448,64]{1,2,0:T(8,128)(2,1)} async-done(((bf16[1,448,64]{1,2,0:T(8,128)(2,1)}), bf16[32,448,64]{1,2,0:T(8,128)(2,1)}) %all-gather.32.cloned.1.call-update) | async-done | bytes 1835024 | tf_op jit(solution)/shard_map/all_gather | solution.py:54
  553.1 6.0 select_dynamic-update-slice_fusion
  565.2 49.9 %all-gather.24.cloned.1.call-done = bf16[64,8192]{1,0:T(8,128)(2,1)} async-done(((bf16[64,256]{1,0:T(8,128)(2,1)}), bf16[64,8192]{1,0:T(8,128)(2,1)}) %all-gather.24.cloned.1.call-update) | async-done | bytes 1048592 | tf_op jit(solution)/shard_map/all_gather | solution.py:46
  616.6 5.7 fusion.26
  622.3 6.0 fusion.49
  629.0 47.5 %all-gather.34.cloned.1.call-done = bf16[32,448,64]{1,2,0:T(8,128)(2,1)} async-done(((bf16[1,448,64]{1,2,0:T(8,128)(2,1)}), bf16[32,448,64]{1,2,0:T(8,128)(2,1)}) %all-gather.34.cloned.1.call-update) | async-done | bytes 1835024 | tf_op jit(solution)/shard_map/all_gather | solution.py:54
  682.6 6.6 fusion.52
  (86 shorter events, 68.4 us)
Async XLA Ops:
  6.5 88.8 %all-gather.16.cloned.1.call-start = ((), (), s32[]{:S(2)}) async-start(), calls=%async_computation | async-start | bytes 1081344 | tf_op jit(solution)/shard_map/all_gather | solution.py:46
  7.9 150.6 %all-gather.26.cloned.1.call-start = ((), (), s32[]{:S(2)}) async-start(), calls=%async_computation.5 | async-start | bytes 2162688 | tf_op jit(solution)/shard_map/all_gather | solution.py:54
  75.3 21.6 %copy-start.6 = (f32[1,8192]{1,0:T(1,128)S(1)}, f32[1,8192]{1,0:T(1,128)}, u32[]{:S(2)}) copy-start(f32[1,8192]{1,0:T(1,128)} %param.8) | copy-start | bytes 98308
  96.9 5.8 copy-start
  96.9 5.8 copy-start.1
  102.7 3.2 copy-start.13
  105.7 121.0 %all-gather.18.cloned.1.call-start = ((), (), s32[]{:S(2)}) async-start(), calls=%async_computation.1 | async-start | bytes 1081344 | tf_op jit(solution)/shard_map/all_gather | solution.py:46
  161.3 3.4 copy-start.12
  164.7 11.2 %copy-start.7 = (bf16[128,256]{1,0:T(8,128)(2,1)S(1)}, bf16[128,256]{1,0:T(8,128)(2,1)}, u32[]{:S(2)}) copy-start(bf16[128,256]{1,0:T(8,128)(2,1)} %param.7) | copy-start | bytes 196612
  170.7 5.2 collective-permute-start
  176.5 111.6 %all-gather.28.cloned.1.call-start = ((), (), s32[]{:S(2)}) async-start(), calls=%async_computation.6 | async-start | bytes 2162688 | tf_op jit(solution)/shard_map/all_gather | solution.py:54
  228.2 5.7 copy-start.3
  239.9 116.2 %all-gather.20.cloned.1.call-start = ((), (), s32[]{:S(2)}) async-start(), calls=%async_computation.2 | async-start | bytes 1081344 | tf_op jit(solution)/shard_map/all_gather | solution.py:46
  290.8 3.4 copy-start.10
  300.2 5.2 collective-permute-start.1
  306.0 111.6 %all-gather.30.cloned.1.call-start = ((), (), s32[]{:S(2)}) async-start(), calls=%async_computation.7 | async-start | bytes 2162688 | tf_op jit(solution)/shard_map/all_gather | solution.py:54
  357.6 5.7 copy-start.4
  369.4 116.2 %all-gather.22.cloned.1.call-start = ((), (), s32[]{:S(2)}) async-start(), calls=%async_computation.3 | async-start | bytes 1081344 | tf_op jit(solution)/shard_map/all_gather | solution.py:46
  420.3 3.4 copy-start.11
  429.7 5.2 collective-permute-start.2
  435.5 111.6 %all-gather.32.cloned.1.call-start = ((), (), s32[]{:S(2)}) async-start(), calls=%async_computation.8 | async-start | bytes 2162688 | tf_op jit(solution)/shard_map/all_gather | solution.py:54
  487.1 5.7 copy-start.5
  498.8 116.2 %all-gather.24.cloned.1.call-start = ((), (), s32[]{:S(2)}) async-start(), calls=%async_computation.4 | async-start | bytes 1081344 | tf_op jit(solution)/shard_map/all_gather | solution.py:46
  549.8 3.4 copy-start.9
  559.1 5.2 collective-permute-start.3
  565.0 111.6 %all-gather.34.cloned.1.call-start = ((), (), s32[]{:S(2)}) async-start(), calls=%async_computation.9 | async-start | bytes 2162688 | tf_op jit(solution)/shard_map/all_gather | solution.py:54
  616.6 5.7 copy-start.2
  679.3 3.4 copy-start.8
Sparse Core Ops, SparseCore 0:
  9.8 51.9 all-gather.15
  105.8 52.7 all-gather.25
  176.6 49.9 all-gather.17
  240.0 48.0 all-gather.27
  306.1 49.9 all-gather.19
  369.5 48.0 all-gather.29
  435.6 49.9 all-gather.21
  499.0 48.0 all-gather.31
  565.1 49.9 all-gather.23
  628.4 48.0 all-gather.33
where the time goes:
time: 708 us; the launch traced here: 696 us
  waiting for transfers between devices  403 us (57%)
  local copies, waits for them, and re-layouts  139 us (20%)
  matrix products  111 us (16%)
  starting transfers between devices  18 us (3%)
  between operations  14 us (2%)
  other arithmetic  11.5 us (2%)
    all_gather x5, waiting for transfers between devices, local(): whole = lax.all_gather(incoming, 'tensor', axis=1, tiled=True)  200 us
    all_gather x5, waiting for transfers between devices, local(): lax.all_gather(section_hidden, 'tensor', axis=1, tiled=True)  199 us
    reshape x3, local copies, waits for them, and re-layouts, densify(): jnp.transpose(dense, (1, 2, 0, 3)).reshape(row_blocks * BS, tile_count * BS)  58.6 us
    transpose x3, local copies, waits for them, and re-layouts, densify(): jnp.transpose(dense, (1, 2, 0, 3)).reshape(row_blocks * BS, tile_count * BS)  48.6 us
    dot_general x5, matrix products, local(): jnp.dot(lax.all_gather(section_hidden, 'tensor', axis=1, tiled=True), dow...  30.6 us
    dot_general x5, matrix products, local(): jnp.dot(section_normed, gate_dense, preferred_element_type=jnp.float32)  28.7 us
    dot_general x5, matrix products, local(): jnp.dot(section_normed, up_dense, preferred_element_type=jnp.float32)  26.7 us
    dot_general x3, matrix products, densify(): jnp.einsum('crm,cmq->crq', picks, blocks, preferred_element_type=jnp.bflo...  24.9 us
  transfers between devices with their start and end apart: 14, of which 13 were waited for; matrix products, arithmetic and copies ran while one was open for 19% of the time, Pallas kernels for 0%

commit v1 on v0

--- a/solution.py
+++ b/solution.py
@@ -43,7 +43,9 @@
         first_group = min(tick_now, group_count - 1)
         first_rows = x_in[first_group * rows_micro : (first_group + 1) * rows_micro]
         incoming = jnp.where(segment_at == 0, first_rows, carried)
-        whole = lax.all_gather(incoming, "tensor", axis=1, tiled=True)
+        whole = jnp.concatenate(
+            lax.all_to_all(jnp.stack([incoming] * lax.axis_size("tensor")), "tensor", 0, 0), axis=1
+        )
         wide = whole.astype(jnp.float32)
         stat = jnp.mean(wide * wide, axis=1, keepdims=True)
         section_normed = (wide * lax.rsqrt(stat + 1e-05) * gain_row[None, :]).astype(jnp.bfloat16)

time: 708 us -> 587 us (0.83)
  waiting for transfers between devices: 403 us -> 204 us
  blocking collectives: 0 us -> 93.4 us
  matrix products: 111 us -> 84.9 us
  local copies, waits for them, and re-layouts: 139 us -> 153 us
  starting transfers between devices: 18 us -> 25.7 us
    all_gather x5 -> x0, waiting for transfers between devices: 200 us -> none  [local(): whole = lax.all_gather(incoming, 'tensor', axis=1, tiled=True)]
    all_to_all x0 -> x4, blocking collectives: none -> 93.4 us  [local(): lax.all_to_all(jnp.stack([incoming] * lax.axis_size('tensor')), 'tensor',...]
    dot_general x5, matrix products: 28.7 us -> 14.6 us  [local(): jnp.dot(section_normed, gate_dense, preferred_element_type=jnp.float32)]
    dot_general x5, matrix products: 26.7 us -> 14.3 us  [local(): jnp.dot(section_normed, up_dense, preferred_element_type=jnp.float32)]
    all_to_all x0 -> x1, starting transfers between devices: none -> 8.58 us  [local(): lax.all_to_all(jnp.stack([incoming] * lax.axis_size('tensor')), 'tensor',...]
    unnamed x35 -> x48, local copies, waits for them, and re-layouts: 18.1 us -> 24.5 us
  transfers between devices with their start and end apart: 14 -> 10, of which waited for: 13 -> 9; matrix products, arithmetic and copies ran while one was open for 19% -> 23% of each run, Pallas kernels for 0% -> 0%
where the time goes in v1:
time: 587 us; the launch traced here: 580 us
  waiting for transfers between devices  204 us (35%)
  local copies, waits for them, and re-layouts  153 us (26%)
  blocking collectives  93.4 us (16%)
  matrix products  84.9 us (14%)
  starting transfers between devices  25.7 us (4%)
  between operations  14 us (2%)
    all_gather x5, waiting for transfers between devices, local(): lax.all_gather(section_hidden, 'tensor', axis=1, tiled=True)  200 us
    all_to_all x4, blocking collectives, local(): lax.all_to_all(jnp.stack([incoming] * lax.axis_size('tensor')), 'tensor',...  93.4 us
    reshape x3, local copies, waits for them, and re-layouts, densify(): jnp.transpose(dense, (1, 2, 0, 3)).reshape(row_blocks * BS, tile_count * BS)  58.6 us
    transpose x3, local copies, waits for them, and re-layouts, densify(): jnp.transpose(dense, (1, 2, 0, 3)).reshape(row_blocks * BS, tile_count * BS)  48.6 us
    dot_general x5, matrix products, local(): jnp.dot(lax.all_gather(section_hidden, 'tensor', axis=1, tiled=True), dow...  31.1 us
    dot_general x3, matrix products, densify(): jnp.einsum('crm,cmq->crq', picks, blocks, preferred_element_type=jnp.bflo...  24.9 us
    unnamed x48, local copies, waits for them, and re-layouts  24.5 us
    all_gather x5, local copies, waits for them, and re-layouts, local(): lax.all_gather(section_hidden, 'tensor', axis=1, tiled=True)  19.2 us
  transfers between devices with their start and end apart: 10, of which 9 were waited for; matrix products, arithmetic and copies ran while one was open for 23% of the time, Pallas kernels for 0%

profile of v1, /device:TPU:1, one launch (start us, length us, event | category | flops | bytes accessed | tf_op | source)
XLA Modules:
  0.0 580.4 jit_solution(6819437583407962879)
XLA Ops:
  8.4 8.6 %all-to-all-start = ((bf16[32,64,256]{2,1,0:T(8,128)(2,1)}), bf16[32,64,256]{2,1,0:T(8,128)(2,1)S(1)}, u32[]{:S(2)}, u32[]{:S(2)}) async-start(bf16[32,64,256]{2,1,0:T(8,128)(2,1)} %stack.10), calls=%async_computation | async-start | bytes 2097152 | tf_op jit(solution)/shard_map/all_to_all | solution.py:47
  19.7 7.7 %fusion.4 = bf16[7,128,4096]{1,2,0:T(8,128)(2,1)} fusion(bf16[1,7,72,4096]{3,2,1,0:T(8,128)(2,1)} %param.10, s32[7,72]{1,0:T(8,128)S(1)} %bitcast.150), kind=kOutput, calls=%fused_computation.4 | convolution fusion | flops 528546816 | bytes 11470816 | tf_op jit(solution)/shard_map/crm,cmq->crq/dot_general | solution.py:22
  27.4 15.7 %copy.23 = bf16[128,64,7,64]{1,0,3,2:T(8,128)(2,1)} copy(bf16[128,64,7,64]{0,3,1,2:T(8,128)(2,1)} %bitcast.137) | data formatting | bytes 14680064 | tf_op jit(solution)/shard_map/transpose | solution.py:24
  43.2 20.0 %reshape.193 = bf16[8192,448]{0,1:T(8,128)(2,1)} reshape(bf16[128,64,7,64]{1,0,3,2:T(8,128)(2,1)} %copy.23) | data formatting | bytes 14680064 | tf_op jit(solution)/shard_map/reshape | solution.py:24
  63.2 7.7 %fusion.2 = bf16[7,128,4096]{1,2,0:T(8,128)(2,1)} fusion(bf16[1,7,72,4096]{3,2,1,0:T(8,128)(2,1)} %param.11, s32[7,72]{1,0:T(8,128)S(1)} %bitcast.151), kind=kOutput, calls=%fused_computation.2 | convolution fusion | flops 528546816 | bytes 11470816 | tf_op jit(solution)/shard_map/crm,cmq->crq/dot_general | solution.py:22
  70.9 15.6 %copy.25 = bf16[128,64,7,64]{1,0,3,2:T(8,128)(2,1)} copy(bf16[128,64,7,64]{0,3,1,2:T(8,128)(2,1)} %bitcast.136) | data formatting | bytes 14680064 | tf_op jit(solution)/shard_map/transpose | solution.py:24
  86.5 20.0 %reshape.195 = bf16[8192,448]{0,1:T(8,128)(2,1)} reshape(bf16[128,64,7,64]{1,0,3,2:T(8,128)(2,1)} %copy.25) | data formatting | bytes 14680064 | tf_op jit(solution)/shard_map/reshape | solution.py:24
  107.2 5.7 fusion.43
  116.1 9.5 %fusion = bf16[4,224,4096]{1,2,0:T(8,128)(2,1)} fusion(bf16[4,126,4096]{2,0,1:T(4,128)(2,1)} %bitcast.138, s32[4,126]{1,0:T(4,128)S(1)} %bitcast.152), kind=kOutput, calls=%fused_computation | convolution fusion | flops 924956928 | bytes 11470816 | tf_op jit(solution)/shard_map/crm,cmq->crq/dot_general | solution.py:22
  125.6 17.3 %copy.29 = bf16[224,64,4,64]{1,0,3,2:T(8,128)(2,1)} copy(bf16[224,64,4,64]{0,3,1,2:T(8,128)(2,1)} %bitcast.135) | data formatting | bytes 14680064 | tf_op jit(solution)/shard_map/transpose | solution.py:24
  142.9 18.5 %reshape.197 = bf16[14336,256]{0,1:T(8,128)(2,1)} reshape(bf16[224,64,4,64]{1,0,3,2:T(8,128)(2,1)} %copy.29) | data formatting | bytes 14680064 | tf_op jit(solution)/shard_map/reshape | solution.py:24
  161.4 6.1 %all-gather.11.cloned.1.call-done = bf16[32,448,64]{1,2,0:T(8,128)(2,1)} async-done(((bf16[1,448,64]{1,2,0:T(8,128)(2,1)}), bf16[32,448,64]{1,2,0:T(8,128)(2,1)}) %all-gather.11.cloned.1.call-update) | async-done | bytes 1835024 | tf_op jit(solution)/shard_map/all_gather | solution.py:56
  171.7 4.8 reshape.199
  176.5 6.1 %select_dynamic-update-slice_fusion.3 = (bf16[128,256]{1,0:T(8,128)(2,1)S(1)}, bf16[64,256]{1,0:T(8,128)(2,1)S(1)}) fusion(bf16[128,256]{1,0:T(8,128)(2,1)S(1)} %broadcast_in_dim.6, s32[]{:T(128)S(6)} %select_n.77, pred[]{:T(512)S(6)} %and.16, bf16[14336,64]{0,1:T(8,128)(2,1)} %reshape.199, bf16[14336,256]{0,1:T(8,128)(2,1)} %reshape.197, ...), kind=kOutput, calls=%fused_computation.68 | convolution fusion | flops 469827584 | bytes 9273349 | tf_op jit(solution)/shard_map/dot_general | solution.py:55
  182.7 4.2 collective-permute-start
  188.0 23.5 %all_to_all.25 = bf16[32,64,256]{2,1,0:T(8,128)(2,1)S(1)} all-to-all(bf16[32,64,256]{2,1,0:T(8,128)(2,1)S(1)} %stack.11), channel_id=1, replica_groups=mesh['replica'=2,'segment'=4,'tensor'=32] {'tensor'}, dimensions={0} | all-to-all | bytes 2097152 | tf_op jit(solution)/shard_map/all_to_all | solution.py:47
  217.5 48.6 %all-gather.13.cloned.1.call-done = bf16[32,448,64]{1,2,0:T(8,128)(2,1)} async-done(((bf16[1,448,64]{1,2,0:T(8,128)(2,1)}), bf16[32,448,64]{1,2,0:T(8,128)(2,1)}) %all-gather.13.cloned.1.call-update) | async-done | bytes 1835024 | tf_op jit(solution)/shard_map/all_gather | solution.py:56
  270.2 4.8 reshape.201
  275.0 6.1 %select_dynamic-update-slice_fusion.2 = (bf16[128,256]{1,0:T(8,128)(2,1)S(1)}, bf16[64,256]{1,0:T(8,128)(2,1)S(1)}) fusion(bf16[128,256]{1,0:T(8,128)(2,1)S(1)} %get-tuple-element.11, s32[]{:T(128)S(6)} %select_n.80, pred[]{:T(512)S(6)} %and.17, bf16[64,256]{1,0:T(8,128)(2,1)S(1)} %broadcast_select_fusion.3, bf16[14336,64]{0,1:T(8,128)(2,1)} %reshape.201, ...), kind=kOutput, calls=%fused_computation.67 | convolution fusion | flops 469827584 | bytes 9306117 | tf_op jit(solution)/shard_map/dot_general | solution.py:55
  281.1 4.2 collective-permute-start.1
  286.5 23.2 %all_to_all.26 = bf16[32,64,256]{2,1,0:T(8,128)(2,1)S(1)} all-to-all(bf16[32,64,256]{2,1,0:T(8,128)(2,1)S(1)} %stack.12), channel_id=1, replica_groups=mesh['replica'=2,'segment'=4,'tensor'=32] {'tensor'}, dimensions={0} | all-to-all | bytes 2097152 | tf_op jit(solution)/shard_map/all_to_all | solution.py:47
  315.7 48.6 %all-gather.15.cloned.1.call-done = bf16[32,448,64]{1,2,0:T(8,128)(2,1)} async-done(((bf16[1,448,64]{1,2,0:T(8,128)(2,1)}), bf16[32,448,64]{1,2,0:T(8,128)(2,1)}) %all-gather.15.cloned.1.call-update) | async-done | bytes 1835024 | tf_op jit(solution)/shard_map/all_gather | solution.py:56
  368.4 4.8 reshape.203
  373.3 6.1 %select_dynamic-update-slice_fusion.1 = (bf16[128,256]{1,0:T(8,128)(2,1)S(1)}, bf16[64,256]{1,0:T(8,128)(2,1)S(1)}) fusion(bf16[128,256]{1,0:T(8,128)(2,1)S(1)} %get-tuple-element.9, s32[]{:T(128)S(6)} %select_n.84, pred[]{:T(512)S(6)} %and.18, bf16[64,256]{1,0:T(8,128)(2,1)S(1)} %broadcast_select_fusion.2, bf16[14336,64]{0,1:T(8,128)(2,1)} %reshape.203, ...), kind=kOutput, calls=%fused_computation.66 | convolution fusion | flops 469827584 | bytes 9306117 | tf_op jit(solution)/shard_map/dot_general | solution.py:55
  379.4 4.2 collective-permute-start.2
  384.7 23.3 %all_to_all.27 = bf16[32,64,256]{2,1,0:T(8,128)(2,1)S(1)} all-to-all(bf16[32,64,256]{2,1,0:T(8,128)(2,1)S(1)} %stack.13), channel_id=1, replica_groups=mesh['replica'=2,'segment'=4,'tensor'=32] {'tensor'}, dimensions={0} | all-to-all | bytes 2097152 | tf_op jit(solution)/shard_map/all_to_all | solution.py:47
  414.0 48.6 %all-gather.17.cloned.1.call-done = bf16[32,448,64]{1,2,0:T(8,128)(2,1)} async-done(((bf16[1,448,64]{1,2,0:T(8,128)(2,1)}), bf16[32,448,64]{1,2,0:T(8,128)(2,1)}) %all-gather.17.cloned.1.call-update) | async-done | bytes 1835024 | tf_op jit(solution)/shard_map/all_gather | solution.py:56
  466.7 4.8 reshape.205
  471.5 6.1 %select_dynamic-update-slice_fusion = (bf16[128,256]{1,0:T(8,128)(2,1)S(1)}, bf16[64,256]{1,0:T(8,128)(2,1)S(1)}) fusion(bf16[128,256]{1,0:T(8,128)(2,1)S(1)} %get-tuple-element.7, s32[]{:T(128)S(6)} %select_n.88, pred[]{:T(512)S(6)} %and.19, bf16[64,256]{1,0:T(8,128)(2,1)S(1)} %broadcast_select_fusion.1, bf16[14336,64]{0,1:T(8,128)(2,1)} %reshape.205, ...), kind=kOutput, calls=%fused_computation.65 | convolution fusion | flops 469827584 | bytes 9306117 | tf_op jit(solution)/shard_map/dot_general | solution.py:55
  483.0 23.3 %all_to_all.28 = bf16[32,64,256]{2,1,0:T(8,128)(2,1)S(1)} all-to-all(bf16[32,64,256]{2,1,0:T(8,128)(2,1)S(1)} %stack.14), channel_id=1, replica_groups=mesh['replica'=2,'segment'=4,'tensor'=32] {'tensor'}, dimensions={0} | all-to-all | bytes 2097152 | tf_op jit(solution)/shard_map/all_to_all | solution.py:47
  512.9 48.0 %all-gather.19.cloned.1.call-done = bf16[32,448,64]{1,2,0:T(8,128)(2,1)} async-done(((bf16[1,448,64]{1,2,0:T(8,128)(2,1)}), bf16[32,448,64]{1,2,0:T(8,128)(2,1)}) %all-gather.19.cloned.1.call-update) | async-done | bytes 1835024 | tf_op jit(solution)/shard_map/all_gather | solution.py:56
  567.0 6.6 %fusion.42 = bf16[1,128,256]{2,1,0:T(8,128)(2,1)} fusion(bf16[1,128,256]{2,1,0:T(8,128)(2,1)} %copy.55, s32[]{:T(128)S(6)} %select_n.92, bf16[64,256]{1,0:T(8,128)(2,1)S(1)} %broadcast_select_fusion, bf16[128,256]{1,0:T(8,128)(2,1)S(1)} %get-tuple-element.5, pred[]{:T(512)S(6)} %and.20, bf16[14336,64]{0,1:T(8,128)(2,1)} %reshape.207, ...), kind=kOutput, calls=%fused_computation.64 | convolution fusion | flops 469827584 | bytes 9273349 | tf_op jit(solution)/shard_map/dot_general | solution.py:55
  (116 shorter events, 63.9 us)
Async XLA Ops:
  8.4 98.1 %all-to-all-start = ((bf16[32,64,256]{2,1,0:T(8,128)(2,1)}), bf16[32,64,256]{2,1,0:T(8,128)(2,1)S(1)}, u32[]{:S(2)}, u32[]{:S(2)}) async-start(bf16[32,64,256]{2,1,0:T(8,128)(2,1)} %stack.10), calls=%async_computation | async-start | bytes 2097152 | tf_op jit(solution)/shard_map/all_to_all | solution.py:47
  17.0 150.6 %all-gather.11.cloned.1.call-start = ((), (), s32[]{:S(2)}) async-start(), calls=%async_computation.5 | async-start | bytes 2162688 | tf_op jit(solution)/shard_map/all_gather | solution.py:56
  106.5 6.5 %slice-start.8 = ((s8[7340032]{0:T(1024)(128)(4,1)}), s8[4194304]{0:T(1024)(128)(4,1)S(1)}, s32[]{:S(2)}) async-start(s8[7340032]{0:T(1024)(128)(4,1)} %bitcast.125), calls=%async_computation.18 | async-start | bytes 8388608
  107.2 5.7 slice-start.9
  113.0 3.2 copy-start.1
  115.9 150.2 %all-gather.13.cloned.1.call-start = ((), (), s32[]{:S(2)}) async-start(), calls=%async_computation.6 | async-start | bytes 2162688 | tf_op jit(solution)/shard_map/all_gather | solution.py:56
  171.7 40.6 %slice-start = ((s8[7340032]{0:T(1024)(128)(4,1)}), s8[3145728]{0:T(1024)(128)(4,1)S(1)}, s32[]{:S(2)}) async-start(s8[7340032]{0:T(1024)(128)(4,1)} %bitcast.117), calls=%async_computation.10 | async-start | bytes 6291456
  176.5 11.3 %copy-start = (bf16[128,256]{1,0:T(8,128)(2,1)S(1)}, bf16[128,256]{1,0:T(8,128)(2,1)}, u32[]{:S(2)}) copy-start(bf16[128,256]{1,0:T(8,128)(2,1)} %param.7) | copy-start | bytes 196612
  176.5 35.7 %slice-start.1 = ((s8[7340032]{0:T(1024)(128)(4,1)}), s8[4194304]{0:T(1024)(128)(4,1)S(1)}, s32[]{:S(2)}) async-start(s8[7340032]{0:T(1024)(128)(4,1)} %bitcast.117), calls=%async_computation.11 | async-start | bytes 8388608
  182.7 5.2 collective-permute-start
  188.0 26.5 %slice-start.10 = ((s8[7340032]{0:T(1024)(128)(4,1)}), s8[4194304]{0:T(1024)(128)(4,1)S(1)}, s32[]{:S(2)}) async-start(s8[7340032]{0:T(1024)(128)(4,1)} %bitcast.127), calls=%async_computation.20 | async-start | bytes 8388608
  212.3 2.3 slice-start.11
  217.4 146.9 %all-gather.15.cloned.1.call-start = ((), (), s32[]{:S(2)}) async-start(), calls=%async_computation.7 | async-start | bytes 2162688 | tf_op jit(solution)/shard_map/all_gather | solution.py:56
  270.2 40.3 %slice-start.2 = ((s8[7340032]{0:T(1024)(128)(4,1)}), s8[3145728]{0:T(1024)(128)(4,1)S(1)}, s32[]{:S(2)}) async-start(s8[7340032]{0:T(1024)(128)(4,1)} %bitcast.119), calls=%async_computation.12 | async-start | bytes 6291456
  275.0 35.5 %slice-start.3 = ((s8[7340032]{0:T(1024)(128)(4,1)}), s8[4194304]{0:T(1024)(128)(4,1)S(1)}, s32[]{:S(2)}) async-start(s8[7340032]{0:T(1024)(128)(4,1)} %bitcast.119), calls=%async_computation.13 | async-start | bytes 8388608
  281.1 5.2 collective-permute-start.1
  286.5 26.3 %slice-start.12 = ((s8[7340032]{0:T(1024)(128)(4,1)}), s8[4194304]{0:T(1024)(128)(4,1)S(1)}, s32[]{:S(2)}) async-start(s8[7340032]{0:T(1024)(128)(4,1)} %bitcast.129), calls=%async_computation.22 | async-start | bytes 8388608
  310.5 2.2 slice-start.13
  315.7 147.0 %all-gather.17.cloned.1.call-start = ((), (), s32[]{:S(2)}) async-start(), calls=%async_computation.8 | async-start | bytes 2162688 | tf_op jit(solution)/shard_map/all_gather | solution.py:56
  368.4 40.3 %slice-start.4 = ((s8[7340032]{0:T(1024)(128)(4,1)}), s8[3145728]{0:T(1024)(128)(4,1)S(1)}, s32[]{:S(2)}) async-start(s8[7340032]{0:T(1024)(128)(4,1)} %bitcast.121), calls=%async_computation.14 | async-start | bytes 6291456
  373.2 35.5 %slice-start.5 = ((s8[7340032]{0:T(1024)(128)(4,1)}), s8[4194304]{0:T(1024)(128)(4,1)S(1)}, s32[]{:S(2)}) async-start(s8[7340032]{0:T(1024)(128)(4,1)} %bitcast.121), calls=%async_computation.15 | async-start | bytes 8388608
  379.4 5.2 collective-permute-start.2
  384.7 26.3 %slice-start.14 = ((s8[7340032]{0:T(1024)(128)(4,1)}), s8[4194304]{0:T(1024)(128)(4,1)S(1)}, s32[]{:S(2)}) async-start(s8[7340032]{0:T(1024)(128)(4,1)} %bitcast.131), calls=%async_computation.24 | async-start | bytes 8388608
  408.8 2.3 slice-start.15
  413.9 147.0 %all-gather.19.cloned.1.call-start = ((), (), s32[]{:S(2)}) async-start(), calls=%async_computation.9 | async-start | bytes 2162688 | tf_op jit(solution)/shard_map/all_gather | solution.py:56
  466.7 40.4 %slice-start.6 = ((s8[7340032]{0:T(1024)(128)(4,1)}), s8[3145728]{0:T(1024)(128)(4,1)S(1)}, s32[]{:S(2)}) async-start(s8[7340032]{0:T(1024)(128)(4,1)} %bitcast.123), calls=%async_computation.16 | async-start | bytes 6291456
  471.5 35.6 %slice-start.7 = ((s8[7340032]{0:T(1024)(128)(4,1)}), s8[4194304]{0:T(1024)(128)(4,1)S(1)}, s32[]{:S(2)}) async-start(s8[7340032]{0:T(1024)(128)(4,1)} %bitcast.123), calls=%async_computation.17 | async-start | bytes 8388608
  477.7 5.2 collective-permute-start.3
  483.0 26.4 %slice-start.16 = ((s8[7340032]{0:T(1024)(128)(4,1)}), s8[4194304]{0:T(1024)(128)(4,1)S(1)}, s32[]{:S(2)}) async-start(s8[7340032]{0:T(1024)(128)(4,1)} %bitcast.133), calls=%async_computation.26 | async-start | bytes 8388608
  507.1 2.3 slice-start.17
Sparse Core Ops, SparseCore 0:
  116.0 51.5 all-gather.10
  217.5 48.5 all-gather.12
  315.8 48.5 all-gather.14
  414.1 48.5 all-gather.16
  512.4 48.5 all-gather.18
